TPU v7x, 32 devices: a whole 2x2x4 slice. The times are simulated.
32 devices in a mesh: gx: 8 (over z, x), gy: 4 (over y, core).
Axes of the slice: x: 2, y: 2, z: 4, core: 2. Of those that a mesh axis runs over, the one named last changes fastest.
Arguments:
- right_side: float32 [4096, 128], P(('gx', 'gy'))
- compress: float32 [4096, 128], P(('gx', 'gy')), may hold values from 0.5 to 8
- block_fill: int32 [4096], P(('gx', 'gy')), may hold values from 32 to 128, as said below
- pair_home: int32 [12288], P(('gx', 'gy')), may hold values from 0 to 4095, as said below
- pair_far: int32 [12288], P(('gx', 'gy')), may hold values from 0 to 4095, as said below
- pair_count: int32 [32], P(('gx', 'gy')), may hold values from 1 to 384, as said below
- weights: bfloat16 [12288, 128, 128], P(('gx', 'gy')), may hold values from 0 to 0.015625
Outputs:
- solution_field: float32 [4096, 128], P(('gx', 'gy'))
- residual: float32 [4096, 128], P(('gx', 'gy'))
Inputs may be any that keep to these rules, and one draw needn't show every extreme that they name: `pair_home`: pair slot s names as first block a block of device s // 384, blocks of device d being d * 128 to d * 128 + 127, devices numbered gx major. `pair_far`: the second block belongs to the slot's device or to one of its eight neighbours on the periodic gx by gy grid of devices. `pair_count`: slots after a device's count are ignored; some devices hold 384. `block_fill`: slots after a block's fill are padding; some block holds 128.
All inputs are finite; a program needn't handle non-finite values.
Results may differ from a plain program's by a relative error of at most 0.015.
Values may be sent and summed in bfloat16 or wider, within the bound.
A program may use at most 64 MiB of HBM per device.

v0:
```python
import functools

import jax
import jax.numpy as jnp
from jax import lax
from jax.experimental import pallas as pl
from jax.experimental.pallas import tpu as pltpu
from jax.sharding import PartitionSpec as P

ITERS = 3
GROUP = 16
MESH = pl.DeviceIdType.MESH
F32 = jnp.float32
BF16 = jnp.bfloat16


def matmul(a, b):
    return jnp.dot(a, b, preferred_element_type=F32)


def halves(value):
    high = value.astype(BF16)
    return high, (value - high.astype(F32)).astype(BF16)


def kernel(
    sizes,
    right_ref,
    compress_ref,
    fill_ref,
    index_ref,
    weights_hbm,
    x_ref,
    r_ref,
    wv,
    onehot_home_t,
    onehot_home,
    onehot_far_t,
    onehot_far,
    mask,
    live,
    degree,
    gathered,
    rows_out,
    rows_sum,
    local,
    w_now,
    nearby,
    give,
    take,
    give_deg,
    take_deg,
    red_y,
    red_x,
    load_sem,
    halo_send,
    halo_recv,
    ret_send,
    ret_recv,
    deg_send,
    deg_recv,
    ry_send,
    ry_recv,
    rx_send,
    rx_recv,
):
    n_x, n_y, chunks = sizes
    blocks, tile = right_ref.shape
    npairs = weights_hbm.shape[0]
    groups = npairs // GROUP
    per_chunk = npairs // chunks
    my_x = lax.axis_index("gx")
    my_y = lax.axis_index("gy")

    loads = [
        pltpu.make_async_copy(
            weights_hbm.at[pl.ds(i * per_chunk, per_chunk)],
            wv.at[pl.ds(i * per_chunk, per_chunk)],
            load_sem.at[i],
        )
        for i in range(chunks)
    ]
    for load in loads:
        load.start()

    def at(dx, dy):
        return (lax.rem(my_x + dx + n_x, n_x), lax.rem(my_y + dy + n_y, n_y))

    friends = {(dx % n_x, dy % n_y) for dx in (-1, 0, 1) for dy in (-1, 0, 1)}
    friends |= {(0, dy) for dy in range(n_y)} | {(dx, 0) for dx in range(n_x)}
    friends = sorted(friends - {(0, 0)})
    barrier = pltpu.get_barrier_semaphore()
    for dx, dy in friends:
        pl.semaphore_signal(barrier, inc=1, device_id=at(dx, dy), device_id_type=MESH)

    around = [n for n in range(9) if n != 4]

    def send(n, src, dst, ssem, rsem):
        return pltpu.make_async_remote_copy(
            src_ref=src,
            dst_ref=dst,
            send_sem=ssem,
            recv_sem=rsem,
            device_id=at(n // 3 - 1, n % 3 - 1),
            device_id_type=MESH,
        )

    def halo(k):
        return [
            send(n, nearby.at[k, 4], nearby.at[k, 8 - n], halo_send.at[k, n], halo_recv.at[k, 8 - n])
            for n in around
        ]

    def returns(k):
        return [
            send(n, give.at[k, n], take.at[k, 8 - n], ret_send.at[k, n], ret_recv.at[k, 8 - n])
            for n in around
        ]

    def degrees():
        return [
            send(n, give_deg.at[n], take_deg.at[8 - n], deg_send.at[n], deg_recv.at[8 - n])
            for n in around
        ]

    fill = jnp.broadcast_to(fill_ref[...].astype(F32), (tile, blocks)).T
    live_now = (lax.broadcasted_iota(jnp.int32, (blocks, tile), 1).astype(F32) < fill).astype(F32)
    live[...] = live_now
    nearby[0, 4] = (live_now * right_ref[...]).astype(BF16)

    pl.semaphore_wait(barrier, len(friends))
    for copy in halo(0):
        copy.start()

    home_row = jnp.broadcast_to(index_ref[0:1, :], (blocks, npairs))
    far_row = jnp.broadcast_to(index_ref[1:2, :], (blocks, npairs))
    which = lax.broadcasted_iota(jnp.int32, (blocks, npairs), 0)
    pick = jnp.where(which == home_row, 1.0, 0.0)
    onehot_home_t[...] = pick.astype(BF16)
    onehot_home[...] = pick.T.astype(BF16)
    for n in range(9):
        pick = jnp.where(which + n * blocks == far_row, 1.0, 0.0)
        onehot_far_t[n * blocks : (n + 1) * blocks, :] = pick.astype(BF16)
        onehot_far[:, n * blocks : (n + 1) * blocks] = pick.T.astype(BF16)
    for p in range(GROUP):
        own = lax.broadcasted_iota(jnp.int32, (GROUP, tile), 0) == p
        mask[:, p * tile : (p + 1) * tile] = jnp.where(own, 1.0, 0.0)

    def group_tiles(g):
        return wv[pl.ds(g * GROUP, GROUP)].reshape(GROUP * tile, tile)

    def rows(g):
        return pl.ds(pl.multiple_of(g * GROUP, GROUP), GROUP)

    def backward_group(first, g, carry):
        x = gathered[rows(g), :]
        spread = mask[...].astype(BF16)
        lhs = jnp.concatenate([x] * GROUP, axis=1) * spread
        if first:
            lhs = jnp.concatenate([lhs, spread], axis=0)
        out = matmul(lhs, group_tiles(g))
        rows_out[rows(g), :] = out[:GROUP]
        if first:
            rows_sum[rows(g), :] = out[GROUP:]
        return carry

    def diagonal(y):
        total = y[:, :tile] * mask[:, :tile]
        for p in range(1, GROUP):
            part = slice(p * tile, (p + 1) * tile)
            total += y[:, part] * mask[:, part]
        return total

    def toward_group(first, g, carry):
        x = gathered[rows(g), :]
        if first:
            x = jnp.concatenate([x, jnp.ones_like(x)], axis=0)
        y = lax.dot_general(
            x, group_tiles(g), (((1,), (1,)), ((), ())), preferred_element_type=F32
        )
        rows_out[rows(g), :] = diagonal(y[:GROUP])
        if first:
            rows_sum[rows(g), :] = diagonal(y[GROUP:])
        return carry

    def scatter(selector, values):
        high, low = halves(values)
        return matmul(selector, high) + matmul(selector, low)

    def operate(k, field, during=None):
        first = k == 0
        gathered[...] = matmul(onehot_home[...], nearby[k, 4]).astype(BF16)
        if first:
            per = groups // chunks
            for i in range(chunks):
                loads[i].wait()
                lax.fori_loop(
                    i * per, (i + 1) * per, functools.partial(backward_group, True), 0, unroll=2
                )
            sums = halves(rows_sum[...])
            for n in range(9):
                select = onehot_far_t[n * blocks : (n + 1) * blocks, :]
                total = matmul(select, sums[0]) + matmul(select, sums[1])
                if n == 4:
                    degree[...] = total
                else:
                    give_deg[n] = total.astype(BF16)
            for copy in degrees():
                copy.start()
        else:
            lax.fori_loop(0, groups, functools.partial(backward_group, False), 0, unroll=2)
        terms = rows_out[...].astype(BF16)
        for n in range(9):
            total = matmul(onehot_far_t[n * blocks : (n + 1) * blocks, :], terms)
            if n == 4:
                local[...] = total
            else:
                give[k, n] = total.astype(BF16)
        for copy in returns(k):
            copy.start()
        if during is not None:
            during()
        for copy in halo(k):
            copy.wait_recv()
        gathered[...] = matmul(onehot_far[...], nearby[k].reshape(9 * blocks, tile)).astype(BF16)
        lax.fori_loop(0, groups, functools.partial(toward_group, first), 0, unroll=2)
        if first:
            degree[...] += scatter(onehot_home_t[...], rows_sum[...])
        total = local[...] + matmul(onehot_home_t[...], rows_out[...].astype(BF16))
        if first:
            for copy in degrees():
                copy.wait_recv()
            for n in around:
                degree[...] += take_deg[n].astype(F32)
        for copy in returns(k):
            copy.wait_recv()
        for n in around:
            total += take[k, n].astype(F32)
        pairs = degree[...] * nearby[k, 4].astype(F32) - total
        return compress_ref[...] * field + live[...] * pairs

    def sum_y(k):
        return [
            pltpu.make_async_remote_copy(
                src_ref=red_y.at[k, my_y],
                dst_ref=red_y.at[k, my_y],
                send_sem=ry_send.at[k, d],
                recv_sem=ry_recv.at[k, n_y - d],
                device_id=at(0, d),
                device_id_type=MESH,
            )
            for d in range(1, n_y)
        ]

    def sum_x(k):
        return [
            pltpu.make_async_remote_copy(
                src_ref=red_x.at[k, my_x],
                dst_ref=red_x.at[k, my_x],
                send_sem=rx_send.at[k, d],
                recv_sem=rx_recv.at[k, n_x - d],
                device_id=at(d, 0),
                device_id_type=MESH,
            )
            for d in range(1, n_x)
        ]

    def sums_start(k, residual, image):
        which_row = lax.broadcasted_iota(jnp.int32, (8, tile), 0)
        norm = jnp.sum(residual * residual, axis=0, keepdims=True)
        along = jnp.sum(residual * image, axis=0, keepdims=True)
        red_y[k, my_y] = jnp.where(which_row == 0, norm, jnp.where(which_row == 1, along, 0.0))
        for copy in sum_y(k):
            copy.start()

    def sums_middle(k):
        for copy in sum_y(k):
            copy.wait_recv()
        red_x[k, my_x] = jnp.sum(red_y[k], axis=0)
        for copy in sum_x(k):
            copy.start()

    def sums_end(k):
        for copy in sum_x(k):
            copy.wait_recv()
        totals = jnp.sum(jnp.sum(red_x[k], axis=0), axis=1, keepdims=True)
        return totals[0:1, :], totals[1:2, :]

    residual = right_ref[...]
    image = operate(0, residual)
    w_now[...] = image
    r_ref[...] = residual
    norm_before = alpha = direction = along = onward = None
    for k in range(ITERS):
        last = k + 1 == ITERS
        sums_start(k, r_ref[...], w_now[...])
        if not last:
            nearby[k + 1, 4] = (live[...] * w_now[...]).astype(BF16)
            for copy in halo(k + 1):
                copy.start()
            further = operate(k + 1, w_now[...], lambda: sums_middle(k))
        else:
            sums_middle(k)
        norm_now, product = sums_end(k)
        residual = r_ref[...]
        image = w_now[...]
        if k == 0:
            alpha = norm_now / product
            direction, along = residual, image
            x_ref[...] = alpha * direction
            if not last:
                onward = further
        else:
            ratio = norm_now / norm_before
            alpha = norm_now / (product - ratio * norm_now / alpha)
            direction = residual + ratio * direction
            along = image + ratio * along
            x_ref[...] += alpha * direction
            if not last:
                onward = further + ratio * onward
        norm_before = norm_now
        r_ref[...] = residual - alpha * along
        if not last:
            w_now[...] = image - alpha * onward

    for k in range(ITERS):
        for copy in halo(k) + returns(k) + sum_y(k) + sum_x(k):
            copy.wait_send()
    for copy in degrees():
        copy.wait_send()


def on_device(mesh_sizes, right_side, compress, block_fill, pair_home, pair_far, pair_count, weights):
    n_x, n_y = mesh_sizes
    blocks, tile = right_side.shape
    npairs = weights.shape[0]
    my_x = lax.axis_index("gx")
    my_y = lax.axis_index("gy")
    keep = jnp.arange(npairs, dtype=jnp.int32) < pair_count[0]
    far_device = pair_far // blocks
    slot_x = (far_device // n_y - my_x + 1) % n_x
    slot_y = (far_device % n_y - my_y + 1) % n_y
    far_slot = (slot_x * 3 + slot_y) * blocks + pair_far % blocks
    home = pair_home - (my_x * n_y + my_y) * blocks
    index = jnp.where(keep, jnp.stack([home, far_slot]), -1)
    chunks = 4
    dma = pltpu.SemaphoreType.DMA
    vmem = pl.BlockSpec(memory_space=pltpu.VMEM)
    out = jax.ShapeDtypeStruct((blocks, tile), F32)
    return pl.pallas_call(
        functools.partial(kernel, (n_x, n_y, chunks)),
        out_shape=(out, out),
        in_specs=[vmem, vmem, vmem, vmem, pl.BlockSpec(memory_space=pl.ANY)],
        out_specs=(vmem, vmem),
        scratch_shapes=[
            pltpu.VMEM((npairs, tile, tile), BF16),
            pltpu.VMEM((blocks, npairs), BF16),
            pltpu.VMEM((npairs, blocks), BF16),
            pltpu.VMEM((9 * blocks, npairs), BF16),
            pltpu.VMEM((npairs, 9 * blocks), BF16),
            pltpu.VMEM((GROUP, GROUP * tile), F32),
            pltpu.VMEM((blocks, tile), F32),
            pltpu.VMEM((blocks, tile), F32),
            pltpu.VMEM((npairs, tile), BF16),
            pltpu.VMEM((npairs, tile), F32),
            pltpu.VMEM((npairs, tile), F32),
            pltpu.VMEM((blocks, tile), F32),
            pltpu.VMEM((blocks, tile), F32),
            pltpu.VMEM((ITERS, 9, blocks, tile), BF16),
            pltpu.VMEM((ITERS, 9, blocks, tile), BF16),
            pltpu.VMEM((ITERS, 9, blocks, tile), BF16),
            pltpu.VMEM((9, blocks, tile), BF16),
            pltpu.VMEM((9, blocks, tile), BF16),
            pltpu.VMEM((ITERS, n_y, 8, tile), F32),
            pltpu.VMEM((ITERS, n_x, 8, tile), F32),
            dma((chunks,)),
            dma((ITERS, 9)),
            dma((ITERS, 9)),
            dma((ITERS, 9)),
            dma((ITERS, 9)),
            dma((9,)),
            dma((9,)),
            dma((ITERS, n_y)),
            dma((ITERS, n_y)),
            dma((ITERS, n_x)),
            dma((ITERS, n_x)),
        ],
        compiler_params=pltpu.CompilerParams(
            collective_id=0, has_side_effects=True, vmem_limit_bytes=56 * 1024 * 1024
        ),
    )(right_side, compress, block_fill[None], index, weights)


def solution(mesh):
    return jax.shard_map(
        functools.partial(on_device, (mesh.shape["gx"], mesh.shape["gy"])),
        mesh=mesh,
        in_specs=(
            P(("gx", "gy"), None),
            P(("gx", "gy"), None),
            P(("gx", "gy")),
            P(("gx", "gy")),
            P(("gx", "gy")),
            P(("gx", "gy")),
            P(("gx", "gy"), None, None),
        ),
        out_specs=(P(("gx", "gy"), None), P(("gx", "gy"), None)),
        check_vma=False,
    )
```

profile of v0, /device:TPU:0, one launch (start us, length us, event | category | flops | bytes accessed | tf_op | source)
XLA Modules:
  0.0 64.4 jit_solution(15912607129162915500)
XLA Ops:
  1.3 0.7 %fusion.6 = s32[384]{0:T(512)S(1)} fusion(s32[384]{0:T(512)} %param.11, s32[]{:T(128)S(6)} %axis_index.25, s32[]{:T(128)S(6)} %axis_index.23), kind=kLoop, calls=%fused_computation.23 | loop fusion | flops 26112 | bytes 3080 | tf_op jit(solution)/shard_map/add | solution.py:343
  2.0 0.7 %broadcast_subtract_fusion = s32[384]{0:T(512)S(1)} fusion(s32[384]{0:T(512)} %param.10, s32[]{:T(128)S(6)} %mul.15), kind=kLoop, calls=%fused_computation.32 | loop fusion | flops 384 | bytes 3076 | tf_op jit(solution)/shard_map/sub | solution.py:344
  2.7 0.6 add_select_fusion.index_ref
  3.3 58.2 %shard_map.86 = (f32[128,128]{1,0:T(8,128)}, f32[128,128]{1,0:T(8,128)}) custom-call(f32[128,128]{1,0:T(8,128)} %right_ref.1, f32[128,128]{1,0:T(8,128)} %compress_ref.1, s32[1,128]{1,0:T(1,128)} %bitcast.3, s32[2,384]{1,0:T(2,128)} %add_select_fusion.index_ref, bf16[384,128,128]{2,1,0:T(8,128)(2,1)} %weights_hbm.1), custom_call_target="tpu_custom_call" | custom-call | tf_op jit(solution)/shard_map/pallas_call | solution.py:350
  61.5 1.5 %copy.12 = f32[128,128]{1,0:T(8,128)} copy(f32[128,128]{1,0:T(8,128)} %get-tuple-element.4) | data formatting | bytes 131072
  63.0 1.5 %copy.13 = f32[128,128]{1,0:T(8,128)} copy(f32[128,128]{1,0:T(8,128)} %get-tuple-element.5) | data formatting | bytes 131072
  (3 shorter events, 0.0 us)
where the time goes:
time: 64.8 us; the launch traced here: 64.4 us
  Pallas kernels  58.2 us (90%)
  local copies, waits for them, and re-layouts  2.96 us (5%)
  other arithmetic  2 us (3%)
  between operations  1.3 us (2%)
    pallas_call x1, Pallas kernels, on_device(): pl.pallas_call(functools.partial(kernel, (n_x, n_y, chunks)), out_shape=(...  58.2 us
    unnamed x2, local copies, waits for them, and re-layouts  2.95 us

commit v1 on v0

--- a/solution.py
+++ b/solution.py
@@ -9,6 +9,7 @@
 
 ITERS = 3
 GROUP = 16
+UNROLL = 3
 MESH = pl.DeviceIdType.MESH
 F32 = jnp.float32
 BF16 = jnp.bfloat16
@@ -28,11 +29,14 @@
     right_ref,
     compress_ref,
     fill_ref,
-    index_ref,
+    home_ref,
+    far_ref,
+    count_ref,
     weights_hbm,
     x_ref,
     r_ref,
     wv,
+    wt,
     onehot_home_t,
     onehot_home,
     onehot_far_t,
@@ -48,6 +52,7 @@
     nearby,
     give,
     take,
+    far_deg,
     give_deg,
     take_deg,
     red_y,
@@ -93,34 +98,37 @@
     for dx, dy in friends:
         pl.semaphore_signal(barrier, inc=1, device_id=at(dx, dy), device_id_type=MESH)
 
-    around = [n for n in range(9) if n != 4]
-
-    def send(n, src, dst, ssem, rsem):
+    longer = 2 * lax.rem(my_x, 2) - 1
+    order = [(longer, dy) for dy in (1, -1, 0)] + [(-longer, dy) for dy in (1, -1, 0)]
+    order += [(0, 1), (0, -1)]
+    around = [((dx + 1) * 3 + dy + 1, dx, dy) for dx, dy in order]
+
+    def send(to, src, dst, ssem, rsem):
         return pltpu.make_async_remote_copy(
             src_ref=src,
             dst_ref=dst,
             send_sem=ssem,
             recv_sem=rsem,
-            device_id=at(n // 3 - 1, n % 3 - 1),
+            device_id=at(to[1], to[2]),
             device_id_type=MESH,
         )
 
     def halo(k):
         return [
-            send(n, nearby.at[k, 4], nearby.at[k, 8 - n], halo_send.at[k, n], halo_recv.at[k, 8 - n])
-            for n in around
+            send(to, nearby.at[k, 4], nearby.at[k, 8 - to[0]], halo_send.at[k, to[0]], halo_recv.at[k, 8 - to[0]])
+            for to in around
         ]
 
     def returns(k):
         return [
-            send(n, give.at[k, n], take.at[k, 8 - n], ret_send.at[k, n], ret_recv.at[k, 8 - n])
-            for n in around
+            send(to, give.at[k, to[0]], take.at[k, 8 - to[0]], ret_send.at[k, to[0]], ret_recv.at[k, 8 - to[0]])
+            for to in around
         ]
 
     def degrees():
         return [
-            send(n, give_deg.at[n], take_deg.at[8 - n], deg_send.at[n], deg_recv.at[8 - n])
-            for n in around
+            send(to, give_deg.at[to[0]], take_deg.at[8 - to[0]], deg_send.at[to[0]], deg_recv.at[8 - to[0]])
+            for to in around
         ]
 
     fill = jnp.broadcast_to(fill_ref[...].astype(F32), (tile, blocks)).T
@@ -132,60 +140,41 @@
     for copy in halo(0):
         copy.start()
 
-    home_row = jnp.broadcast_to(index_ref[0:1, :], (blocks, npairs))
-    far_row = jnp.broadcast_to(index_ref[1:2, :], (blocks, npairs))
+    keep = lax.broadcasted_iota(jnp.int32, (1, npairs), 1) < count_ref[0]
+    home_row = jnp.broadcast_to(jnp.where(keep, home_ref[...], -1), (blocks, npairs))
+    far_row = jnp.broadcast_to(jnp.where(keep, far_ref[...], -1), (blocks, npairs))
     which = lax.broadcasted_iota(jnp.int32, (blocks, npairs), 0)
-    pick = jnp.where(which == home_row, 1.0, 0.0)
+    pick = jnp.where(which + (my_x * n_y + my_y) * blocks == home_row, 1.0, 0.0)
     onehot_home_t[...] = pick.astype(BF16)
     onehot_home[...] = pick.T.astype(BF16)
     for n in range(9):
-        pick = jnp.where(which + n * blocks == far_row, 1.0, 0.0)
+        far_x, far_y = at(n // 3 - 1, n % 3 - 1)
+        pick = jnp.where(which + (far_x * n_y + far_y) * blocks == far_row, 1.0, 0.0)
         onehot_far_t[n * blocks : (n + 1) * blocks, :] = pick.astype(BF16)
         onehot_far[:, n * blocks : (n + 1) * blocks] = pick.T.astype(BF16)
     for p in range(GROUP):
         own = lax.broadcasted_iota(jnp.int32, (GROUP, tile), 0) == p
-        mask[:, p * tile : (p + 1) * tile] = jnp.where(own, 1.0, 0.0)
-
-    def group_tiles(g):
-        return wv[pl.ds(g * GROUP, GROUP)].reshape(GROUP * tile, tile)
+        mask[:, p * tile : (p + 1) * tile] = jnp.where(own, 1.0, 0.0).astype(BF16)
 
     def rows(g):
         return pl.ds(pl.multiple_of(g * GROUP, GROUP), GROUP)
 
-    def backward_group(first, g, carry):
+    def group_products(first, held, g, carry):
         x = gathered[rows(g), :]
-        spread = mask[...].astype(BF16)
+        spread = mask[...]
         lhs = jnp.concatenate([x] * GROUP, axis=1) * spread
         if first:
             lhs = jnp.concatenate([lhs, spread], axis=0)
-        out = matmul(lhs, group_tiles(g))
-        rows_out[rows(g), :] = out[:GROUP]
+        out = matmul(lhs, held[pl.ds(g * GROUP, GROUP)].reshape(GROUP * tile, tile))
+        rows_out[rows(g), :] = out[:GROUP].astype(BF16)
         if first:
             rows_sum[rows(g), :] = out[GROUP:]
         return carry
 
-    def diagonal(y):
-        total = y[:, :tile] * mask[:, :tile]
-        for p in range(1, GROUP):
-            part = slice(p * tile, (p + 1) * tile)
-            total += y[:, part] * mask[:, part]
-        return total
-
-    def toward_group(first, g, carry):
-        x = gathered[rows(g), :]
-        if first:
-            x = jnp.concatenate([x, jnp.ones_like(x)], axis=0)
-        y = lax.dot_general(
-            x, group_tiles(g), (((1,), (1,)), ((), ())), preferred_element_type=F32
-        )
-        rows_out[rows(g), :] = diagonal(y[:GROUP])
-        if first:
-            rows_sum[rows(g), :] = diagonal(y[GROUP:])
-        return carry
-
-    def scatter(selector, values):
-        high, low = halves(values)
-        return matmul(selector, high) + matmul(selector, low)
+    def turned_products(g, carry):
+        for p in range(GROUP):
+            wt[g * GROUP + p] = wv[g * GROUP + p].T
+        return group_products(True, wt, g, carry)
 
     def operate(k, field, during=None):
         first = k == 0
@@ -195,46 +184,61 @@
             for i in range(chunks):
                 loads[i].wait()
                 lax.fori_loop(
-                    i * per, (i + 1) * per, functools.partial(backward_group, True), 0, unroll=2
+                    i * per,
+                    (i + 1) * per,
+                    functools.partial(group_products, True, wv),
+                    0,
+                    unroll=UNROLL,
                 )
-            sums = halves(rows_sum[...])
+            high, low = halves(rows_sum[...])
             for n in range(9):
                 select = onehot_far_t[n * blocks : (n + 1) * blocks, :]
-                total = matmul(select, sums[0]) + matmul(select, sums[1])
-                if n == 4:
-                    degree[...] = total
-                else:
-                    give_deg[n] = total.astype(BF16)
-            for copy in degrees():
-                copy.start()
+                far_deg[n] = matmul(select, high) + matmul(select, low)
+                give_deg[n] = far_deg[n].astype(BF16)
+            for copy in halo(k):
+                copy.wait_recv()
         else:
-            lax.fori_loop(0, groups, functools.partial(backward_group, False), 0, unroll=2)
-        terms = rows_out[...].astype(BF16)
-        for n in range(9):
+            lax.fori_loop(
+                0, groups, functools.partial(group_products, False, wv), 0, unroll=UNROLL
+            )
+        terms = rows_out[...]
+        for n in (0, 1, 2, 6, 7, 8, 3, 5, 4):
             total = matmul(onehot_far_t[n * blocks : (n + 1) * blocks, :], terms)
+            if first and n != 4:
+                total -= far_deg[n] * nearby[k, n].astype(F32)
             if n == 4:
                 local[...] = total
             else:
                 give[k, n] = total.astype(BF16)
         for copy in returns(k):
             copy.start()
+        if first:
+            for copy in degrees():
+                copy.start()
         if during is not None:
             during()
-        for copy in halo(k):
-            copy.wait_recv()
+        if not first:
+            for copy in halo(k):
+                copy.wait_recv()
         gathered[...] = matmul(onehot_far[...], nearby[k].reshape(9 * blocks, tile)).astype(BF16)
-        lax.fori_loop(0, groups, functools.partial(toward_group, first), 0, unroll=2)
         if first:
-            degree[...] += scatter(onehot_home_t[...], rows_sum[...])
-        total = local[...] + matmul(onehot_home_t[...], rows_out[...].astype(BF16))
-        if first:
+            lax.fori_loop(0, groups, turned_products, 0)
+            high, low = halves(rows_sum[...])
+            select = onehot_home_t[...]
+            degree[...] = far_deg[4] + matmul(select, high) + matmul(select, low)
+        else:
+            lax.fori_loop(
+                0, groups, functools.partial(group_products, False, wt), 0, unroll=UNROLL
+            )
+        total = local[...] + matmul(onehot_home_t[...], rows_out[...])
+        if k == 1:
             for copy in degrees():
                 copy.wait_recv()
-            for n in around:
+            for n in (0, 1, 2, 3, 5, 6, 7, 8):
                 degree[...] += take_deg[n].astype(F32)
         for copy in returns(k):
             copy.wait_recv()
-        for n in around:
+        for n in (0, 1, 2, 3, 5, 6, 7, 8):
             total += take[k, n].astype(F32)
         pairs = degree[...] * nearby[k, 4].astype(F32) - total
         return compress_ref[...] * field + live[...] * pairs
@@ -334,15 +338,6 @@
     n_x, n_y = mesh_sizes
     blocks, tile = right_side.shape
     npairs = weights.shape[0]
-    my_x = lax.axis_index("gx")
-    my_y = lax.axis_index("gy")
-    keep = jnp.arange(npairs, dtype=jnp.int32) < pair_count[0]
-    far_device = pair_far // blocks
-    slot_x = (far_device // n_y - my_x + 1) % n_x
-    slot_y = (far_device % n_y - my_y + 1) % n_y
-    far_slot = (slot_x * 3 + slot_y) * blocks + pair_far % blocks
-    home = pair_home - (my_x * n_y + my_y) * blocks
-    index = jnp.where(keep, jnp.stack([home, far_slot]), -1)
     chunks = 4
     dma = pltpu.SemaphoreType.DMA
     vmem = pl.BlockSpec(memory_space=pltpu.VMEM)
@@ -350,25 +345,27 @@
     return pl.pallas_call(
         functools.partial(kernel, (n_x, n_y, chunks)),
         out_shape=(out, out),
-        in_specs=[vmem, vmem, vmem, vmem, pl.BlockSpec(memory_space=pl.ANY)],
+        in_specs=[vmem] * 5 + [pl.BlockSpec(memory_space=pltpu.SMEM), pl.BlockSpec(memory_space=pl.ANY)],
         out_specs=(vmem, vmem),
         scratch_shapes=[
+            pltpu.VMEM((npairs, tile, tile), BF16),
             pltpu.VMEM((npairs, tile, tile), BF16),
             pltpu.VMEM((blocks, npairs), BF16),
             pltpu.VMEM((npairs, blocks), BF16),
             pltpu.VMEM((9 * blocks, npairs), BF16),
             pltpu.VMEM((npairs, 9 * blocks), BF16),
-            pltpu.VMEM((GROUP, GROUP * tile), F32),
+            pltpu.VMEM((GROUP, GROUP * tile), BF16),
             pltpu.VMEM((blocks, tile), F32),
             pltpu.VMEM((blocks, tile), F32),
             pltpu.VMEM((npairs, tile), BF16),
-            pltpu.VMEM((npairs, tile), F32),
+            pltpu.VMEM((npairs, tile), BF16),
             pltpu.VMEM((npairs, tile), F32),
             pltpu.VMEM((blocks, tile), F32),
             pltpu.VMEM((blocks, tile), F32),
             pltpu.VMEM((ITERS, 9, blocks, tile), BF16),
             pltpu.VMEM((ITERS, 9, blocks, tile), BF16),
             pltpu.VMEM((ITERS, 9, blocks, tile), BF16),
+            pltpu.VMEM((9, blocks, tile), F32),
             pltpu.VMEM((9, blocks, tile), BF16),
             pltpu.VMEM((9, blocks, tile), BF16),
             pltpu.VMEM((ITERS, n_y, 8, tile), F32),
@@ -388,7 +385,7 @@
         compiler_params=pltpu.CompilerParams(
             collective_id=0, has_side_effects=True, vmem_limit_bytes=56 * 1024 * 1024
         ),
-    )(right_side, compress, block_fill[None], index, weights)
+    )(right_side, compress, block_fill[None], pair_home[None], pair_far[None], pair_count, weights)
 
 
 def solution(mesh):

time: 64.8 us -> 62.9 us (0.971)
  local copies, waits for them, and re-layouts: 2.96 us -> 5.44 us
  Pallas kernels: 58.2 us -> 55.8 us
  other arithmetic: 2 us -> 0 us
    broadcast_in_dim x0 -> x2, local copies, waits for them, and re-layouts: none -> 2.49 us  [the longest x1 1.25 us: on_device(): pair_home[None]]
    pallas_call x1, Pallas kernels: 58.2 us -> 55.8 us  [on_device(): pl.pallas_call(functools.partial(kernel, (n_x, n_y, chunks)), out_shape=(...]
    add x1 -> x0, other arithmetic: 0.72 us -> none  [on_device(): far_slot = (slot_x * 3 + slot_y) * blocks + pair_far % blocks]
    sub x1 -> x0, other arithmetic: 0.69 us -> none  [on_device(): home = pair_home - (my_x * n_y + my_y) * blocks]
where the time goes in v1:
time: 62.9 us; the launch traced here: 62.5 us
  Pallas kernels  55.8 us (89%)
  local copies, waits for them, and re-layouts  5.44 us (9%)
  between operations  1.29 us (2%)
    pallas_call x1, Pallas kernels, on_device(): pl.pallas_call(functools.partial(kernel, (n_x, n_y, chunks)), out_shape=(...  55.8 us
    unnamed x2, local copies, waits for them, and re-layouts  2.95 us

profile of v1, /device:TPU:0, one launch (start us, length us, event | category | flops | bytes accessed | tf_op | source)
XLA Modules:
  0.0 62.5 jit_solution(250031665231118997)
XLA Ops:
  1.3 1.2 %broadcast_in_dim.10.home_ref = s32[1,384]{1,0:T(1,128)} reshape(s32[384]{0:T(512)} %param.10) | data formatting | bytes 3072 | tf_op jit(solution)/shard_map/broadcast_in_dim | solution.py:388
  2.5 1.2 %broadcast_in_dim.11.far_ref = s32[1,384]{1,0:T(1,128)} reshape(s32[384]{0:T(512)} %param.11) | data formatting | bytes 3072 | tf_op jit(solution)/shard_map/broadcast_in_dim | solution.py:388
  3.8 55.8 %shard_map.86 = (f32[128,128]{1,0:T(8,128)}, f32[128,128]{1,0:T(8,128)}) custom-call(f32[128,128]{1,0:T(8,128)} %right_ref.1, f32[128,128]{1,0:T(8,128)} %compress_ref.1, s32[1,128]{1,0:T(1,128)} %bitcast.1, s32[1,384]{1,0:T(1,128)} %broadcast_in_dim.10.home_ref, s32[1,384]{1,0:T(1,128)} %broadcast_in_dim.11.far_ref, s32[1]{0:T(128)S(6)} %copy.11.count_ref, ...), custom_call_target="tpu_custom_call" | custom-call | tf_op jit(solution)/shard_map/pallas_call | solution.py:345
  59.6 1.5 %copy.12 = f32[128,128]{1,0:T(8,128)} copy(f32[128,128]{1,0:T(8,128)} %get-tuple-element.4) | data formatting | bytes 131072
  61.1 1.5 %copy.13 = f32[128,128]{1,0:T(8,128)} copy(f32[128,128]{1,0:T(8,128)} %get-tuple-element.5) | data formatting | bytes 131072

commit v2 on v1

--- a/solution.py
+++ b/solution.py
@@ -136,10 +136,6 @@
     live[...] = live_now
     nearby[0, 4] = (live_now * right_ref[...]).astype(BF16)
 
-    pl.semaphore_wait(barrier, len(friends))
-    for copy in halo(0):
-        copy.start()
-
     keep = lax.broadcasted_iota(jnp.int32, (1, npairs), 1) < count_ref[0]
     home_row = jnp.broadcast_to(jnp.where(keep, home_ref[...], -1), (blocks, npairs))
     far_row = jnp.broadcast_to(jnp.where(keep, far_ref[...], -1), (blocks, npairs))
@@ -155,6 +151,10 @@
     for p in range(GROUP):
         own = lax.broadcasted_iota(jnp.int32, (GROUP, tile), 0) == p
         mask[:, p * tile : (p + 1) * tile] = jnp.where(own, 1.0, 0.0).astype(BF16)
+
+    pl.semaphore_wait(barrier, len(friends))
+    for copy in halo(0):
+        copy.start()
 
     def rows(g):
         return pl.ds(pl.multiple_of(g * GROUP, GROUP), GROUP)
@@ -210,7 +210,10 @@
                 local[...] = total
             else:
                 give[k, n] = total.astype(BF16)
-        for copy in returns(k):
+            if n == 8:
+                for copy in returns(k)[:6]:
+                    copy.start()
+        for copy in returns(k)[6:]:
             copy.start()
         if first:
             for copy in degrees():
@@ -297,13 +300,15 @@
     norm_before = alpha = direction = along = onward = None
     for k in range(ITERS):
         last = k + 1 == ITERS
-        sums_start(k, r_ref[...], w_now[...])
-        if not last:
+        if last:
+            sums_start(k, r_ref[...], w_now[...])
+        else:
             nearby[k + 1, 4] = (live[...] * w_now[...]).astype(BF16)
             for copy in halo(k + 1):
                 copy.start()
+            sums_start(k, r_ref[...], w_now[...])
             further = operate(k + 1, w_now[...], lambda: sums_middle(k))
-        else:
+        if last:
             sums_middle(k)
         norm_now, product = sums_end(k)
         residual = r_ref[...]

time: 62.9 us -> 62.9 us (level)
  no operation moved by 1% of the time
where the time goes in v2:
time: 62.9 us; the launch traced here: 62.6 us
  Pallas kernels  55.8 us (89%)
  local copies, waits for them, and re-layouts  5.44 us (9%)
  between operations  1.29 us (2%)
    pallas_call x1, Pallas kernels, on_device(): pl.pallas_call(functools.partial(kernel, (n_x, n_y, chunks)), out_shape=(...  55.8 us
    unnamed x2, local copies, waits for them, and re-layouts  2.95 us

profile of v2, /device:TPU:0, one launch (start us, length us, event | category | flops | bytes accessed | tf_op | source)
XLA Modules:
  0.0 62.6 jit_solution(6326800468229537639)
XLA Ops:
  1.3 1.2 %broadcast_in_dim.10.home_ref = s32[1,384]{1,0:T(1,128)} reshape(s32[384]{0:T(512)} %param.10) | data formatting | bytes 3072 | tf_op jit(solution)/shard_map/broadcast_in_dim | solution.py:393
  2.5 1.2 %broadcast_in_dim.11.far_ref = s32[1,384]{1,0:T(1,128)} reshape(s32[384]{0:T(512)} %param.11) | data formatting | bytes 3072 | tf_op jit(solution)/shard_map/broadcast_in_dim | solution.py:393
  3.8 55.8 %shard_map.86 = (f32[128,128]{1,0:T(8,128)}, f32[128,128]{1,0:T(8,128)}) custom-call(f32[128,128]{1,0:T(8,128)} %right_ref.1, f32[128,128]{1,0:T(8,128)} %compress_ref.1, s32[1,128]{1,0:T(1,128)} %bitcast.1, s32[1,384]{1,0:T(1,128)} %broadcast_in_dim.10.home_ref, s32[1,384]{1,0:T(1,128)} %broadcast_in_dim.11.far_ref, s32[1]{0:T(128)S(6)} %copy.11.count_ref, ...), custom_call_target="tpu_custom_call" | custom-call | tf_op jit(solution)/shard_map/pallas_call | solution.py:350
  59.6 1.5 %copy.12 = f32[128,128]{1,0:T(8,128)} copy(f32[128,128]{1,0:T(8,128)} %get-tuple-element.4) | data formatting | bytes 131072
  61.1 1.5 %copy.13 = f32[128,128]{1,0:T(8,128)} copy(f32[128,128]{1,0:T(8,128)} %get-tuple-element.5) | data formatting | bytes 131072
